TPU v7x, 128 devices: a whole 4x4x4 slice. The times are simulated.
128 devices in a mesh: cluster: 16 (over y, x), kshard: 8 (over z, core).
Axes of the slice: x: 4, y: 4, z: 4, core: 2. Of those that a mesh axis runs over, the one named last changes fastest.
Arguments:
- queries: bfloat16 [8192, 768], P('cluster', 'kshard'), may hold values from -24 to 24
- probes: int32 [64, 4], P('cluster'), may hold values from 0 to 15, all different within a row; in each aligned block of 4 rows (0 to 3, 4 to 7, ...) at most 2 rows name the same one
- key_rows: bfloat16 [16, 16384, 768], P('cluster', 'kshard'), may hold values from -8 to 8
- value_rows: bfloat16 [16, 16384, 768], P('cluster', 'kshard'), may hold values from -6 to 6
- key_scale: float32 [16, 128], P('cluster', 'kshard'), may hold values from 0.25 to 3
- key_tiles: int32 [16], P('cluster'), may hold values from 1 to 128, 1024 in all
Outputs:
- joined: bfloat16 [8192, 768], P('cluster', 'kshard')
Inputs may be any that keep to these rules, and one draw needn't show every extreme that they name: `probes`: each row names 4 different clusters; among the tiles of one index of cluster (aligned blocks of 4 tiles) no cluster is named more than 2 times, a bound that some block reaches. `key_tiles`: some cluster has all 128 blocks live.
All inputs are finite; a program needn't handle non-finite values.
Results may differ from a plain program's by a relative error of at most 0.005.
Values may be sent and summed in bfloat16 or wider, within the bound.
A program may use at most 128 MiB of HBM per device.

v0:
```python
import math

import jax
import jax.numpy as jnp
from jax import lax
from jax.sharding import PartitionSpec as P

D = 768
TB = 128
KB = 128


masked_value = -1e30


def combined_all(shard, axis, combine):
    everything = jax.tree.map(lambda part: lax.all_gather(part, axis), shard)
    leading = jax.tree.map(lambda part: part[0], everything)

    def lap(k, so_far):
        return combine(so_far, jax.tree.map(lambda part: part[k], everything))

    return lax.fori_loop(1, lax.axis_size(axis), lap, leading)


def partial_block(query_rows, block_keys, block_values, block_scale, first_row, live_limit):
    products = jnp.dot(query_rows, block_keys.T, preferred_element_type=jnp.float32)
    row_count = products.shape[0]
    scores = (
        products.reshape(row_count, block_scale.shape[0], -1) * block_scale[None, :, None]
    ).reshape(row_count, -1) * (1.0 / math.sqrt(D))
    key_index = first_row + jnp.arange(block_keys.shape[0], dtype=jnp.int32)
    live_keys = (key_index < live_limit)[None, :]
    masked = jnp.where(live_keys, scores, masked_value)
    row_max = jnp.max(masked, axis=1)
    weight = jnp.where(live_keys, jnp.exp(masked - row_max[:, None]), jnp.float32(0.0))
    row_sum = jnp.sum(weight, axis=1)
    mixture = jnp.dot(weight.astype(jnp.bfloat16), block_values, preferred_element_type=jnp.float32)
    return (row_max, row_sum, mixture)


def join_stats(first, second):
    highest = jnp.maximum(first[0], second[0])
    return (
        highest,
        first[1] * jnp.exp(first[0] - highest) + second[1] * jnp.exp(second[0] - highest),
    )


def shards(queries, probes, key_rows, value_rows, key_scale, key_tiles):
    cluster_count = lax.axis_size("cluster")
    tile_count, probe_count = probes.shape
    capacity = max(2, 2 * tile_count * probe_count // cluster_count)
    total_slots = cluster_count * capacity
    column_count = queries.shape[1]
    targets = probes.reshape(-1)
    matches = (targets[:, None] == jnp.arange(cluster_count, dtype=jnp.int32)[None, :]).astype(
        jnp.int32
    )
    before = jnp.cumsum(matches, axis=0) - matches
    slot_index = jnp.sum(before * matches, axis=1)
    position = (targets * capacity + slot_index).reshape(tile_count, probe_count)
    chosen = position[None, :, :] == jnp.arange(total_slots, dtype=jnp.int32)[:, None, None]
    selector = jnp.sum(chosen.astype(jnp.float32), axis=2).astype(jnp.bfloat16)
    gathered = lax.all_gather(queries, "kshard", axis=1, tiled=True)
    packed = jnp.dot(
        selector, gathered.reshape(tile_count, -1), preferred_element_type=jnp.float32
    ).astype(jnp.bfloat16)
    arrived = lax.all_to_all(
        packed.reshape(cluster_count, -1), "cluster", split_axis=0, concat_axis=0, tiled=True
    )
    arrived = arrived.reshape(-1, D)
    slot_rows = arrived.shape[0]
    block_rows = math.gcd(slot_rows, 512)
    first_row = lax.axis_index("kshard") * key_rows.shape[1]
    live_limit = key_tiles[0] * KB
    device_keys = key_rows[0]
    device_values = value_rows[0]
    device_scale = key_scale[0]

    def one_block(query_block):
        return partial_block(
            query_block, device_keys, device_values, device_scale, first_row, live_limit
        )

    row_max, row_sum, mixture = lax.map(
        one_block, arrived.reshape(slot_rows // block_rows, block_rows, D)
    )
    row_max = row_max.reshape(-1)
    row_sum = row_sum.reshape(-1)
    mixture = mixture.reshape(slot_rows, D)
    highest, row_total = combined_all((row_max, row_sum), "kshard", join_stats)
    factor = jnp.exp(row_max - highest)
    columns = lax.psum_scatter(mixture * factor[:, None], "kshard", scatter_dimension=1, tiled=True)
    answer = (columns / row_total[:, None]).astype(jnp.bfloat16)
    carried = lax.optimization_barrier(answer).astype(jnp.float32)
    returned, returned_max, returned_total = (
        lax.all_to_all(
            carried.reshape(cluster_count, -1), "cluster", split_axis=0, concat_axis=0, tiled=True
        ),
        lax.all_to_all(
            highest.reshape(cluster_count, -1), "cluster", split_axis=0, concat_axis=0, tiled=True
        ),
        lax.all_to_all(
            row_total.reshape(cluster_count, -1), "cluster", split_axis=0, concat_axis=0, tiled=True
        ),
    )
    chosen_probe = jnp.transpose(chosen, (2, 1, 0)).astype(jnp.float32)
    highest_precision = lax.Precision.HIGHEST
    fetched = jnp.einsum(
        "ptr,rx->ptx", chosen_probe, returned.reshape(total_slots, -1), precision=highest_precision
    )
    fetched_max = jnp.einsum(
        "ptr,rx->ptx",
        chosen_probe,
        returned_max.reshape(total_slots, -1),
        precision=highest_precision,
    )
    fetched_total = jnp.einsum(
        "ptr,rx->ptx",
        chosen_probe,
        returned_total.reshape(total_slots, -1),
        precision=highest_precision,
    )
    fetched = fetched.reshape(probe_count, tile_count, TB, column_count)
    overall = jnp.max(fetched_max, axis=0)
    weight = jnp.exp(fetched_max - overall[None]) * fetched_total
    joined = jnp.sum(weight[..., None] * fetched, axis=0) / jnp.sum(weight, axis=0)[..., None]
    return joined.reshape(tile_count * TB, column_count).astype(jnp.bfloat16)


def solution(mesh):
    return jax.shard_map(
        shards,
        mesh=mesh,
        in_specs=(
            P("cluster", "kshard"),
            P("cluster", None),
            P("cluster", "kshard", None),
            P("cluster", "kshard", None),
            P("cluster", "kshard"),
            P("cluster"),
        ),
        out_specs=P("cluster", "kshard"),
        check_vma=False,
    )
```

profile of v0, /device:TPU:1, one launch (start us, length us, event | category | flops | bytes accessed | tf_op | source)
XLA Modules:
  0.0 578.7 jit_solution(13691470973580230917)
XLA Ops:
  6.5 16.1 %all_gather.9 = bf16[512,768]{0,1:T(8,128)(2,1)S(1)} all-gather(bf16[512,96]{0,1:T(8,128)(2,1)} %param.10), channel_id=1, replica_groups=mesh['cluster'=16,'kshard'=8] {'kshard'}, dimensions={1}, use_global_device_ids=true | all-gather | bytes 884736 | tf_op jit(solution)/shard_map/all_gather | solution.py:65
  29.2 12.6 %all_to_all.36 = bf16[16,1,196608]{2,1,0:T(2,128)(2,1)} reshape(bf16[32,98304]{1,0:T(8,128)(2,1)} %convolution_convert_fusion) | data formatting | bytes 12582912 | tf_op jit(solution)/shard_map/all_to_all | solution.py:69
  42.4 40.1 %reduce.4 = bf16[16,196608]{1,0:T(8,128)(2,1)} reduce(bf16[16,1,196608]{2,1,0:T(2,128)(2,1)} %all_to_all.36, bf16[]{:T(256)} %broadcast.59), dimensions={1}, to_apply=%all_to_all.36.reduce_sub_computation | reduce | bytes 12582914 | tf_op jit(solution)/shard_map/all_to_all | solution.py:69
  82.4 9.3 %reshape.120 = bf16[16,2,98304]{2,1,0:T(2,128)(2,1)} reshape(bf16[16,196608]{1,0:T(8,128)(2,1)} %reduce.4) | data formatting | bytes 12582912
  91.8 6.8 %all-to-all-start = ((bf16[16,2,98304]{2,1,0:T(2,128)(2,1)}), bf16[16,2,98304]{2,1,0:T(2,128)(2,1)}, u32[]{:S(2)}, u32[]{:S(2)}) async-start(bf16[16,2,98304]{2,1,0:T(2,128)(2,1)} %reshape.120), calls=%async_computation | async-start | bytes 12582912 | tf_op jit(solution)/shard_map/all_to_all | solution.py:69
  99.5 93.1 %all-to-all-done = bf16[16,2,98304]{2,1,0:T(2,128)(2,1)} async-done(((bf16[16,2,98304]{2,1,0:T(2,128)(2,1)}), bf16[16,2,98304]{2,1,0:T(2,128)(2,1)}, u32[]{:S(2)}, u32[]{:S(2)}) %all-to-all-start) | async-done | bytes 6291488 | tf_op jit(solution)/shard_map/all_to_all | solution.py:69
  192.6 14.4 %reshape.121 = bf16[16,1,196608]{2,1,0:T(2,128)(2,1)} reshape(bf16[16,2,98304]{2,1,0:T(2,128)(2,1)} %all-to-all-done) | data formatting | bytes 12582912
  207.0 39.5 %reduce.2 = bf16[16,196608]{1,0:T(8,128)(2,1)} reduce(bf16[16,1,196608]{2,1,0:T(2,128)(2,1)} %reshape.121, bf16[]{:T(256)} %constant.86), dimensions={1}, to_apply=%all_to_all.27.reduce_sub_computation | reduce | bytes 12582914 | tf_op jit(solution)/shard_map/all_to_all | solution.py:69
  246.5 6.4 %reshape_reshape.3 = bf16[8,512,768]{2,1,0:T(8,128)(2,1)} reshape(bf16[16,196608]{1,0:T(8,128)(2,1)} %reduce.2) | data formatting | bytes 12582912 | tf_op jit(solution)/shard_map/reshape;reshape | solution.py:87
  252.9 134.5 %while.31 = (s32[]{:T(128)}, f32[8,512]{1,0:T(8,128)S(1)}, f32[8,512]{1,0:T(8,128)S(1)}, f32[8,512,768]{2,1,0:T(8,128)}, s32[]{:T(128)}, /*index=5*/s32[]{:T(128...) while((s32[]{:T(128)}, f32[8,512]{1,0:T(8,128)S(1)}, ...), condition=%wide.region_6.7_spmd, body=%wide.region_3.6_spmd.sunk | while | flops 3233819648 | bytes 25454812 | solution.py:86
  252.9 6.3 %select_reduce_fusion.5 = (f32[512]{0:T(512)S(1)}, f32[512,16,128]{0,2,1:T(8,128)}) fusion(pred[16,128]{1,0:T(8,128)(4,1)S(1)} %add_compare_fusion.4, f32[16]{0:T(128)S(1)} %bitcast.123, bf16[16,128,768]{2,1,0:T(8,128)(2,1)} %bitcast.121, bf16[8,512,768]{2,1,0:T(8,128)(2,1)} %get-tuple-element.371, s32[]{:T(128)S(6)} %copy.45), kind=kOutput, calls=%fused_computation.7.clone.1 | convolution fusion | flops 1614806528 | bytes 8130628 | tf_op jit(solution)/shard_map/while/body/eval_jaxpr/dot_general | solution.py:27
  264.8 4.9 bitcast_dynamic-update-slice_fusion.2
  269.7 6.3 %select_reduce_fusion.5 = (f32[512]{0:T(512)S(1)}, f32[512,16,128]{0,2,1:T(8,128)}) fusion(pred[16,128]{1,0:T(8,128)(4,1)S(1)} %add_compare_fusion.4, f32[16]{0:T(128)S(1)} %bitcast.123, bf16[16,128,768]{2,1,0:T(8,128)(2,1)} %bitcast.121, bf16[8,512,768]{2,1,0:T(8,128)(2,1)} %get-tuple-element.371, s32[]{:T(128)S(6)} %copy.45), kind=kOutput, calls=%fused_computation.7.clone.1 | convolution fusion | flops 1614806528 | bytes 8130628 | tf_op jit(solution)/shard_map/while/body/eval_jaxpr/dot_general | solution.py:27
  281.6 4.9 bitcast_dynamic-update-slice_fusion.2
  286.5 6.3 %select_reduce_fusion.5 = (f32[512]{0:T(512)S(1)}, f32[512,16,128]{0,2,1:T(8,128)}) fusion(pred[16,128]{1,0:T(8,128)(4,1)S(1)} %add_compare_fusion.4, f32[16]{0:T(128)S(1)} %bitcast.123, bf16[16,128,768]{2,1,0:T(8,128)(2,1)} %bitcast.121, bf16[8,512,768]{2,1,0:T(8,128)(2,1)} %get-tuple-element.371, s32[]{:T(128)S(6)} %copy.45), kind=kOutput, calls=%fused_computation.7.clone.1 | convolution fusion | flops 1614806528 | bytes 8130628 | tf_op jit(solution)/shard_map/while/body/eval_jaxpr/dot_general | solution.py:27
  303.3 6.3 %select_reduce_fusion.5 = (f32[512]{0:T(512)S(1)}, f32[512,16,128]{0,2,1:T(8,128)}) fusion(pred[16,128]{1,0:T(8,128)(4,1)S(1)} %add_compare_fusion.4, f32[16]{0:T(128)S(1)} %bitcast.123, bf16[16,128,768]{2,1,0:T(8,128)(2,1)} %bitcast.121, bf16[8,512,768]{2,1,0:T(8,128)(2,1)} %get-tuple-element.371, s32[]{:T(128)S(6)} %copy.45), kind=kOutput, calls=%fused_computation.7.clone.1 | convolution fusion | flops 1614806528 | bytes 8130628 | tf_op jit(solution)/shard_map/while/body/eval_jaxpr/dot_general | solution.py:27
  315.2 4.9 bitcast_dynamic-update-slice_fusion.2
  320.1 6.3 %select_reduce_fusion.5 = (f32[512]{0:T(512)S(1)}, f32[512,16,128]{0,2,1:T(8,128)}) fusion(pred[16,128]{1,0:T(8,128)(4,1)S(1)} %add_compare_fusion.4, f32[16]{0:T(128)S(1)} %bitcast.123, bf16[16,128,768]{2,1,0:T(8,128)(2,1)} %bitcast.121, bf16[8,512,768]{2,1,0:T(8,128)(2,1)} %get-tuple-element.371, s32[]{:T(128)S(6)} %copy.45), kind=kOutput, calls=%fused_computation.7.clone.1 | convolution fusion | flops 1614806528 | bytes 8130628 | tf_op jit(solution)/shard_map/while/body/eval_jaxpr/dot_general | solution.py:27
  336.9 6.3 %select_reduce_fusion.5 = (f32[512]{0:T(512)S(1)}, f32[512,16,128]{0,2,1:T(8,128)}) fusion(pred[16,128]{1,0:T(8,128)(4,1)S(1)} %add_compare_fusion.4, f32[16]{0:T(128)S(1)} %bitcast.123, bf16[16,128,768]{2,1,0:T(8,128)(2,1)} %bitcast.121, bf16[8,512,768]{2,1,0:T(8,128)(2,1)} %get-tuple-element.371, s32[]{:T(128)S(6)} %copy.45), kind=kOutput, calls=%fused_computation.7.clone.1 | convolution fusion | flops 1614806528 | bytes 8130628 | tf_op jit(solution)/shard_map/while/body/eval_jaxpr/dot_general | solution.py:27
  348.8 5.0 bitcast_dynamic-update-slice_fusion.2
  353.8 6.3 %select_reduce_fusion.5 = (f32[512]{0:T(512)S(1)}, f32[512,16,128]{0,2,1:T(8,128)}) fusion(pred[16,128]{1,0:T(8,128)(4,1)S(1)} %add_compare_fusion.4, f32[16]{0:T(128)S(1)} %bitcast.123, bf16[16,128,768]{2,1,0:T(8,128)(2,1)} %bitcast.121, bf16[8,512,768]{2,1,0:T(8,128)(2,1)} %get-tuple-element.371, s32[]{:T(128)S(6)} %copy.45), kind=kOutput, calls=%fused_computation.7.clone.1 | convolution fusion | flops 1614806528 | bytes 8130628 | tf_op jit(solution)/shard_map/while/body/eval_jaxpr/dot_general | solution.py:27
  365.7 4.9 bitcast_dynamic-update-slice_fusion.2
  370.6 6.3 %select_reduce_fusion.5 = (f32[512]{0:T(512)S(1)}, f32[512,16,128]{0,2,1:T(8,128)}) fusion(pred[16,128]{1,0:T(8,128)(4,1)S(1)} %add_compare_fusion.4, f32[16]{0:T(128)S(1)} %bitcast.123, bf16[16,128,768]{2,1,0:T(8,128)(2,1)} %bitcast.121, bf16[8,512,768]{2,1,0:T(8,128)(2,1)} %get-tuple-element.371, s32[]{:T(128)S(6)} %copy.45), kind=kOutput, calls=%fused_computation.7.clone.1 | convolution fusion | flops 1614806528 | bytes 8130628 | tf_op jit(solution)/shard_map/while/body/eval_jaxpr/dot_general | solution.py:27
  387.4 13.9 %all-gather = f32[8,1,4096]{2,1,0:T(1,128)S(1)} all-gather(f32[1,1,4096]{2,1,0:T(1,128)S(1)} %reshape.100), channel_id=1, replica_groups=mesh['cluster'=16,'kshard'=8] {'kshard'}, dimensions={0}, use_global_device_ids=true | all-gather | bytes 147456 | tf_op jit(solution)/shard_map/all_gather | solution.py:17
  402.0 13.0 %all-gather.1 = f32[8,1,4096]{2,1,0:T(1,128)S(1)} all-gather(f32[1,1,4096]{2,1,0:T(1,128)S(1)} %reshape.102), channel_id=1, replica_groups=mesh['cluster'=16,'kshard'=8] {'kshard'}, dimensions={0}, use_global_device_ids=true | all-gather | bytes 147456 | tf_op jit(solution)/shard_map/all_gather | solution.py:17
  415.7 9.7 %while.32 = (s32[]{:T(128)}, f32[4096]{0:T(1024)}, f32[4096]{0:T(1024)}, f32[8,4096]{1,0:T(8,128)S(1)}, f32[8,4096]{1,0:T(8,128)S(1)}, /*index=5*/s32[]{:T(128)}, s32[]{:T(128)}, s32[]{:T(128)}) while((s32[]{:T(128)}, f32[4096]{0:T(1024)}, f32[4096]{0:T(1024)}, f32[8,4096]{1,0:T(8,128)S(1)}, f32[8,4096]{1,0:T(8,128)S(1)}, ...), condition=%wide.region_8.9_spmd, body=%wide.region_7.8_spmd.sunk | while | flops 24581 | bytes 163971 | solution.py:23
  426.1 9.9 %bitcast_multiply_fusion = f32[4096,768]{1,0:T(8,128)} fusion(f32[8,512,768]{2,1,0:T(8,128)} %get-tuple-element.196, f32[4096]{0:T(1024)S(1)} %subtract_exponential_fusion), kind=kLoop, calls=%fused_computation.18 | loop fusion | flops 3145728 | bytes 25182208 | tf_op jit(solution)/shard_map/mul | solution.py:94
  436.0 12.6 %copy.27 = f32[4096,768]{0,1:T(8,128)} copy(f32[4096,768]{1,0:T(8,128)} %bitcast_multiply_fusion) | data formatting | bytes 25165824
  453.1 66.0 %reduce-scatter.4.cloned.1.call-done = f32[96,4096]{1,0:T(8,128)} async-done(((f32[768,4096]{1,0:T(8,128)}), f32[96,4096]{1,0:T(8,128)}) %reduce-scatter.4.cloned.1.call-update) | async-done | bytes 1572880
  520.9 6.5 %all-to-all-start.1 = ((f32[16,1,256]{2,1,0:T(1,128)}), f32[16,1,256]{2,1,0:T(1,128)S(1)}, u32[]{:S(2)}, u32[]{:S(2)}) async-start(f32[16,1,256]{2,1,0:T(1,128)} %bitcast.16), calls=%async_computation.1 | async-start | bytes 32768 | tf_op jit(solution)/shard_map/all_to_all | solution.py:101
  533.9 5.1 all-to-all-start.3
  539.6 19.9 %all-to-all-done.3 = f32[16,1,24576]{2,1,0:T(1,128)S(1)} async-done(((f32[16,1,24576]{2,1,0:T(1,128)}), f32[16,1,24576]{2,1,0:T(1,128)S(1)}, u32[]{:S(2)}, u32[]{:S(2)}) %all-to-all-start.3) | async-done | bytes 1572896 | tf_op jit(solution)/shard_map/all_to_all | solution.py:98
  (106 shorter events, 104.0 us)
Async XLA Ops:
  91.8 100.8 %all-to-all-start = ((bf16[16,2,98304]{2,1,0:T(2,128)(2,1)}), bf16[16,2,98304]{2,1,0:T(2,128)(2,1)}, u32[]{:S(2)}, u32[]{:S(2)}) async-start(bf16[16,2,98304]{2,1,0:T(2,128)(2,1)} %reshape.120), calls=%async_computation | async-start | bytes 12582912 | tf_op jit(solution)/shard_map/all_to_all | solution.py:69
  98.6 420.5 %reduce-scatter.4.cloned.1.call-start = ((), (), s32[]{:S(2)}) async-start(), calls=%async_computation.5 | async-start | bytes 14155776
  246.5 6.4 %copy-start = (f32[1,16]{1,0:T(1,128)S(1)}, f32[1,16]{1,0:T(1,128)}, u32[]{:S(2)}) copy-start(f32[1,16]{1,0:T(1,128)} %param.14) | copy-start | bytes 196
  448.7 72.2 %all-to-all-start.2 = ((f32[16,1,256]{2,1,0:T(1,128)}), f32[16,1,256]{2,1,0:T(1,128)S(1)}, u32[]{:S(2)}, u32[]{:S(2)}) async-start(f32[16,1,256]{2,1,0:T(1,128)} %bitcast.19), calls=%async_computation.2 | async-start | bytes 32768 | tf_op jit(solution)/shard_map/all_to_all | solution.py:104
  520.9 13.0 %all-to-all-start.1 = ((f32[16,1,256]{2,1,0:T(1,128)}), f32[16,1,256]{2,1,0:T(1,128)S(1)}, u32[]{:S(2)}, u32[]{:S(2)}) async-start(f32[16,1,256]{2,1,0:T(1,128)} %bitcast.16), calls=%async_computation.1 | async-start | bytes 32768 | tf_op jit(solution)/shard_map/all_to_all | solution.py:101
  533.9 25.6 %all-to-all-start.3 = ((f32[16,1,24576]{2,1,0:T(1,128)}), f32[16,1,24576]{2,1,0:T(1,128)S(1)}, u32[]{:S(2)}, u32[]{:S(2)}) async-start(f32[16,1,24576]{2,1,0:T(1,128)} %reshape.115), calls=%async_computation.3 | async-start | bytes 3145728 | tf_op jit(solution)/shard_map/all_to_all | solution.py:98
Sparse Core Ops, SparseCore 0:
  448.8 70.2 reduce-scatter.3
where the time goes:
time: 586 us; the launch traced here: 579 us
  waiting for transfers between devices  180 us (31%)
  other arithmetic  151 us (26%)
  matrix products  96.2 us (16%)
  local copies, waits for them, and re-layouts  70.8 us (12%)
  blocking collectives  43 us (7%)
  starting transfers between devices  23.1 us (4%)
  between operations  14.2 us (2%)
    all_to_all x1, waiting for transfers between devices, shards(): lax.all_to_all(packed.reshape(cluster_count, -1), 'cluster', split_axis=0...  93.1 us
    all_to_all x2, other arithmetic, shards(): lax.all_to_all(packed.reshape(cluster_count, -1), 'cluster', split_axis=0...  79.6 us
    unnamed x2, waiting for transfers between devices  66 us
    dot_general x8, matrix products, partial_block(): jnp.dot(query_rows, block_keys.T, preferred_element_type=jnp.float32)  50.1 us
    dot_general x8, matrix products, partial_block(): jnp.dot(weight.astype(jnp.bfloat16), block_values, preferred_element_type...  39.3 us
    unnamed x11, local copies, waits for them, and re-layouts  38.4 us
    all_gather x2, blocking collectives, combined_all(): everything = jax.tree.map(lambda part: lax.all_gather(part, axis), shard)  26.9 us
    reduce_sum x8, other arithmetic, partial_block(): row_sum = jnp.sum(weight, axis=1)  22 us
  transfers between devices with their start and end apart: 5, of which 4 were waited for; matrix products, arithmetic and copies ran while one was open for 1% of the time, Pallas kernels for 0%

commit v1 on v0

v1 whole, which is shorter than its diff:
```python
import math

import jax
import jax.numpy as jnp
from jax import lax
from jax.experimental import pallas as pl
from jax.experimental.pallas import tpu as pltpu
from jax.sharding import PartitionSpec as P

D = 768
TB = 128
KB = 128
PROBE = 4
TILES = 4
CLUSTERS = 16
CAP = 2
SIDE = 4
SLICE = 96
KEYS = 2048
CHUNK = 1024
HALF = SIDE * SLICE
STAT = 16
PAIRS = CLUSTERS // 2
MASKED = -1e30
MESH = pl.DeviceIdType.MESH
BF16, F32 = jnp.bfloat16, jnp.float32

ORDER = (
    ((1, 1), (3, 3)),
    ((1, 3), (3, 1)),
    ((2, 0), (0, 2)),
    ((1, 2), (3, 0)),
    ((3, 2), (1, 0)),
    ((2, 1), (0, 3)),
    ((2, 3), (0, 1)),
    ((2, 2), (0, 0)),
)


def shifted(cluster, dy, dx):
    return lax.rem(cluster // SIDE + dy, SIDE) * SIDE + lax.rem(lax.rem(cluster, SIDE) + dx, SIDE)


def picked(values, index):
    code = sum(v * 4**i for i, v in enumerate(values))
    return lax.rem(lax.shift_right_logical(jnp.int32(code), 2 * index), 4)


def terms(x):
    high = x.astype(BF16).astype(F32)
    rest = x - high
    middle = rest.astype(BF16).astype(F32)
    low = (rest - middle).astype(BF16).astype(F32)
    row = lax.broadcasted_iota(jnp.int32, (STAT, x.shape[1]), 0)
    return jnp.where(
        row == 0, high, jnp.where(row == 1, middle, jnp.where(row == 2, low, 0.0))
    ).astype(BF16)


def whole(stat):
    s = stat.astype(F32)
    return s[0:1] + s[1:2] + s[2:3]


def joined(parts, logs):
    top = logs[0]
    for x in logs[1:]:
        top = jnp.maximum(top, x)
    total, mass = None, None
    for part, x in zip(parts, logs):
        w = jnp.exp2(x - top)
        term = part.astype(F32) * w
        total = term if total is None else total + term
        mass = w if mass is None else mass + w
    return total / mass, top + jnp.log2(mass)


def kernel(
    q_ref, probes_ref, scale_ref, tiles_ref, k_hbm, v_hbm, out_ref,
    wide, q_t, pack, qbuf, keys, vals, vt, raw, gain, bias, qp, s_a, s_b, acc,
    osend, rbuf, xsend, xbuf,
    load_sem, send_sem, p1_sem, p2_sem, kv_sem, ret_sem, x_sem,
):
    c, k = lax.axis_index("cluster"), lax.axis_index("kshard")
    z, core = k // 2, lax.rem(k, 2)
    other = 1 - core
    sibling = (c, 2 * z + other)

    def column(dz):
        return (c, 2 * lax.rem(z + dz, SIDE) + core)

    k_load = pltpu.make_async_copy(k_hbm.at[0], keys.at[core], load_sem.at[0])
    v_load = pltpu.make_async_copy(v_hbm.at[0], vals, load_sem.at[1])
    k_load.start()
    v_load.start()

    barrier = pltpu.get_barrier_semaphore()

    def greet(i, carry):
        d = lax.rem(2 * c + core + i, 2 * CLUSTERS)
        pl.semaphore_signal(
            barrier, inc=1, device_id=(d // 2, 2 * z + lax.rem(d, 2)), device_id_type=MESH
        )
        return carry

    lax.fori_loop(1, 2 * CLUSTERS, greet, 0)
    for dz in range(1, SIDE):
        pl.semaphore_signal(barrier, inc=1, device_id=column(dz), device_id_type=MESH)

    wide[...] = jnp.zeros_like(wide)
    wide[:, 0:SLICE] = q_ref[...].astype(F32)
    for t in range(TILES):
        q_t[t] = wide[t * TB : (t + 1) * TB, :].T[0:SLICE].astype(BF16)

    def fill(cc, carry):
        seen, first, second = jnp.int32(0), jnp.int32(0), jnp.int32(0)
        for t in range(TILES):
            hit = jnp.int32(0)
            for p in range(PROBE):
                hit = hit + jnp.where(probes_ref[t, p] == cc, 1, 0)
            first = first + t * hit * jnp.where(seen == 0, 1, 0)
            second = second + t * hit * jnp.where(seen == 1, 1, 0)
            seen = seen + hit
        pack[cc, 0] = q_t[first]
        pack[cc, 1] = q_t[second]
        return carry

    lax.fori_loop(0, CLUSTERS, fill, 0)

    for b in range(KEYS // KB):
        raw[core, b : b + 1, :] = jnp.full((1, 2 * TB), scale_ref[0, b], F32)

    pl.semaphore_wait(barrier, 2 * CLUSTERS - 1 + SIDE - 1)

    for i in range(CLUSTERS):
        dy, dx = ORDER[i // 2][i % 2]
        cc = shifted(c, dy, dx)
        for s in range(CAP):
            remote = pltpu.make_async_remote_copy(
                src_ref=pack.at[cc, s], dst_ref=qbuf.at[i, k],
                send_sem=send_sem.at[0], recv_sem=p1_sem.at[i],
                device_id=(cc, 2 * z + s), device_id_type=MESH,
            )
            if dy == 0 and dx == 0:
                @pl.when(core == s)
                def _():
                    pltpu.make_async_copy(pack.at[cc, s], qbuf.at[i, k], p1_sem.at[i]).start()

                @pl.when(core != s)
                def _():
                    remote.start()
            else:
                remote.start()

    k_send = pltpu.make_async_remote_copy(
        src_ref=k_hbm.at[0], dst_ref=keys.at[core], send_sem=kv_sem.at[0],
        recv_sem=kv_sem.at[1], device_id=sibling, device_id_type=MESH,
    )
    k_send.start()
    raw_send = pltpu.make_async_remote_copy(
        src_ref=raw.at[core], dst_ref=raw.at[core], send_sem=kv_sem.at[2],
        recv_sem=kv_sem.at[3], device_id=sibling, device_id_type=MESH,
    )
    raw_send.start()

    v_load.wait()

    def turn(b, carry):
        rows = pl.ds(pl.multiple_of(b * 256, 256), 256)
        vt[core, :, rows] = vals[rows, :].T
        return carry

    lax.fori_loop(0, KEYS // 256, turn, 0)

    def relay(i):
        mine = qbuf.at[i, pl.ds(2 * z, 2)]
        pltpu.make_async_copy(mine, mine, p1_sem.at[i]).wait()
        for dz in (1, 3, 2):
            pltpu.make_async_remote_copy(
                src_ref=mine, dst_ref=mine, send_sem=send_sem.at[1],
                recv_sem=p2_sem.at[i], device_id=column(dz), device_id_type=MESH,
            ).start()

    relay(0)
    relay(1)
    v_send = pltpu.make_async_remote_copy(
        src_ref=vt.at[core], dst_ref=vt.at[core], send_sem=kv_sem.at[4],
        recv_sem=kv_sem.at[5], device_id=sibling, device_id_type=MESH,
    )
    v_send.start()
    relay(2)
    relay(3)

    k_load.wait()
    raw_send.wait()
    block = z * (2 * KEYS // KB) + lax.broadcasted_iota(jnp.int32, (2 * KEYS // KB, 2 * TB), 0)
    live = block < tiles_ref[0]
    flat = raw[...].reshape(2 * KEYS // KB, 2 * TB)
    gain[...] = jnp.where(live, flat * (math.log2(math.e) / math.sqrt(D)), 0.0)
    bias[...] = jnp.where(live, 0.0, MASKED)
    k_send.wait()
    v_send.wait()

    parts = [(h, j) for h in range(2) for j in range(KEYS // CHUNK)]

    def scored(part, s_ref):
        h, j = part
        s = jnp.dot(
            keys[h, j * CHUNK : (j + 1) * CHUNK, :], qp[...], preferred_element_type=F32
        )
        top = None
        for b in range(CHUNK // KB):
            row = (h * KEYS + j * CHUNK) // KB + b
            x = s[b * KB : (b + 1) * KB] * gain[row : row + 1, :] + bias[row : row + 1, :]
            s_ref[b * KB : (b + 1) * KB, :] = x
            high = jnp.max(x, axis=0, keepdims=True)
            top = high if top is None else jnp.maximum(top, high)
        return top

    def visit(pair, carry):
        @pl.when(pair < PAIRS - 2)
        def _():
            relay(2 * pair + 4)
            relay(2 * pair + 5)

        for u in range(2):
            i = 2 * pair + u
            rest = qbuf.at[i, pl.ds(0, 6)]
            pltpu.make_async_copy(rest, rest, p2_sem.at[i]).wait()
            qp[:, u * TB : (u + 1) * TB] = qbuf[i].reshape(D, TB)

        buffers = (s_a, s_b)
        top = scored(parts[0], buffers[0])
        best, mass = None, None
        for n, (h, j) in enumerate(parts):
            if n + 1 < len(parts):
                next_top = scored(parts[n + 1], buffers[(n + 1) % 2])
            now = top if best is None else jnp.maximum(best, top)
            weight = jnp.exp2(buffers[n % 2][...] - now)
            row_sum = jnp.sum(weight, axis=0, keepdims=True)
            mixture = jnp.dot(
                vt[h, :, j * CHUNK : (j + 1) * CHUNK], weight.astype(BF16),
                preferred_element_type=F32,
            )
            if best is None:
                acc[...] = mixture
                mass = row_sum
            else:
                fade = jnp.exp2(best - now)
                acc[...] = acc[...] * fade + mixture
                mass = mass * fade + row_sum
            best = now
            if n + 1 < len(parts):
                top = next_top

        answer = (acc[...] * (1.0 / mass)).astype(BF16)
        logs = terms(best + jnp.log2(mass))
        for u in range(2):
            i = 2 * pair + u
            lanes = slice(u * TB, (u + 1) * TB)
            for half in range(2):
                for part in range(SIDE):
                    first = (2 * part + half) * SLICE
                    osend[i, half, part * SLICE : (part + 1) * SLICE, :] = answer[
                        first : first + SLICE, lanes
                    ]
                osend[i, half, HALF : HALF + STAT, :] = logs[:, lanes]
        for u in range(2):
            i = 2 * pair + u
            dy = picked([(SIDE - ORDER[n][u][0]) % SIDE for n in range(PAIRS)], pair)
            dx = picked([(SIDE - ORDER[n][u][1]) % SIDE for n in range(PAIRS)], pair)
            g = shifted(c, dy, dx)
            for half in range(2):
                here = jnp.logical_and(g == c, core == half)
                source, target = osend.at[i, half], rbuf.at[CAP * c + core]

                @pl.when(here)
                def _():
                    pltpu.make_async_copy(source, target, ret_sem).start()

                @pl.when(jnp.logical_not(here))
                def _():
                    pltpu.make_async_remote_copy(
                        src_ref=source, dst_ref=target, send_sem=send_sem.at[2],
                        recv_sem=ret_sem, device_id=(g, 2 * z + half), device_id_type=MESH,
                    ).start()

        return carry

    lax.fori_loop(0, PAIRS, visit, 0)

    pltpu.make_async_copy(rbuf, rbuf, ret_sem).wait()

    for t in range(TILES):
        found = []
        for p in range(PROBE):
            cc = probes_ref[t, p]
            slot = jnp.int32(0)
            for before in range(t):
                for other_p in range(PROBE):
                    slot = slot + jnp.where(probes_ref[before, other_p] == cc, 1, 0)
            found.append(CAP * cc + slot)
        logs = [whole(rbuf[f, HALF : HALF + STAT, :]) for f in found]
        total, log = joined([rbuf[f, 0:HALF, :] for f in found], logs)
        stat = terms(log)
        for part in range(SIDE):
            xsend[part, t, 0:SLICE, :] = total[part * SLICE : (part + 1) * SLICE].astype(BF16)
            xsend[part, t, SLICE : SLICE + STAT, :] = stat

    for dz in (2, 1, 3):
        pltpu.make_async_remote_copy(
            src_ref=xsend.at[lax.rem(z + dz, SIDE)], dst_ref=xbuf.at[z],
            send_sem=send_sem.at[3], recv_sem=x_sem, device_id=column(dz), device_id_type=MESH,
        ).start()
    xbuf[z] = xsend[z]
    pltpu.make_async_copy(xsend.at[pl.ds(0, 3)], xsend.at[pl.ds(0, 3)], x_sem).wait()

    for t in range(TILES):
        logs = [whole(xbuf[n, t, SLICE : SLICE + STAT, :]) for n in range(SIDE)]
        total, _ = joined([xbuf[n, t, 0:SLICE, :] for n in range(SIDE)], logs)
        tall = jnp.concatenate([total, jnp.zeros((TB - SLICE, TB), F32)], axis=0)
        out_ref[t * TB : (t + 1) * TB, :] = tall.T[:, 0:SLICE].astype(BF16)

    flat_pack = pack.at[pl.ds(0, 15)]
    pltpu.make_async_copy(flat_pack, flat_pack, send_sem.at[0]).wait()
    pltpu.make_async_copy(pack.at[0, 0], pack.at[0, 0], send_sem.at[0]).wait()
    relayed = qbuf.at[pl.ds(0, 12)]
    pltpu.make_async_copy(relayed, relayed, send_sem.at[1]).wait()
    most = osend.at[pl.ds(0, 15)]
    pltpu.make_async_copy(most, most, send_sem.at[2]).wait()
    pltpu.make_async_copy(osend.at[0, 0], osend.at[0, 0], send_sem.at[2]).wait()
    pltpu.make_async_copy(xsend.at[pl.ds(0, 3)], xsend.at[pl.ds(0, 3)], send_sem.at[3]).wait()


def shards(queries, probes, key_rows, value_rows, key_scale, key_tiles):
    vmem = pl.BlockSpec(memory_space=pltpu.VMEM)
    smem = pl.BlockSpec(memory_space=pltpu.SMEM)
    hbm = pl.BlockSpec(memory_space=pl.ANY)
    dma = pltpu.SemaphoreType.DMA
    return pl.pallas_call(
        kernel,
        out_shape=jax.ShapeDtypeStruct((TILES * TB, SLICE), BF16),
        in_specs=[vmem, smem, smem, smem, hbm, hbm],
        out_specs=vmem,
        scratch_shapes=[
            pltpu.VMEM((TILES * TB, TB), F32),
            pltpu.VMEM((TILES, SLICE, TB), BF16),
            pltpu.VMEM((CLUSTERS, CAP, SLICE, TB), BF16),
            pltpu.VMEM((CLUSTERS, 2 * SIDE, SLICE, TB), BF16),
            pltpu.VMEM((2, KEYS, D), BF16),
            pltpu.VMEM((KEYS, D), BF16),
            pltpu.VMEM((2, D, KEYS), BF16),
            pltpu.VMEM((2, KEYS // KB, 2 * TB), F32),
            pltpu.VMEM((2 * KEYS // KB, 2 * TB), F32),
            pltpu.VMEM((2 * KEYS // KB, 2 * TB), F32),
            pltpu.VMEM((D, 2 * TB), BF16),
            pltpu.VMEM((CHUNK, 2 * TB), F32),
            pltpu.VMEM((CHUNK, 2 * TB), F32),
            pltpu.VMEM((D, 2 * TB), F32),
            pltpu.VMEM((CLUSTERS, 2, HALF + STAT, TB), BF16),
            pltpu.VMEM((CAP * CLUSTERS, HALF + STAT, TB), BF16),
            pltpu.VMEM((SIDE, TILES, SLICE + STAT, TB), BF16),
            pltpu.VMEM((SIDE, TILES, SLICE + STAT, TB), BF16),
            dma((2,)),
            dma((4,)),
            dma((CLUSTERS,)),
            dma((CLUSTERS,)),
            dma((6,)),
            dma,
            dma,
        ],
        compiler_params=pltpu.CompilerParams(
            collective_id=0, has_side_effects=True, vmem_limit_bytes=60 * 2**20
        ),
    )(queries, probes, key_scale, key_tiles, key_rows, value_rows)


def solution(mesh):
    return jax.shard_map(
        shards,
        mesh=mesh,
        in_specs=(
            P("cluster", "kshard"),
            P("cluster", None),
            P("cluster", "kshard", None),
            P("cluster", "kshard", None),
            P("cluster", "kshard"),
            P("cluster"),
        ),
        out_specs=P("cluster", "kshard"),
        check_vma=False,
    )
```

time: 586 us -> 78.7 us (0.13); the launches traced: 579 us -> 78.5 us
  waiting for transfers between devices: 180 us -> 0 us
  other arithmetic: 151 us -> 0 us
  matrix products: 96.2 us -> 0 us
  Pallas kernels: 0 us -> 74.5 us
  local copies, waits for them, and re-layouts: 70.8 us -> 3.28 us
  blocking collectives: 43 us -> 0 us
  starting transfers between devices: 23.1 us -> 0 us
  between operations: 14.2 us -> 0.66 us
    all_to_all x4 -> x0, waiting for transfers between devices: 114 us -> none  [the longest x1 93.1 us: shards(): lax.all_to_all(packed.reshape(cluster_count, -1), 'cluster', split_axis=0...]
    dot_general x20 -> x0, matrix products: 96.2 us -> none  [the longest x8 50.1 us: partial_block(): jnp.dot(query_rows, block_keys.T, preferred_element_type=jnp.float32)]
    all_to_all x3 -> x0, other arithmetic: 83.4 us -> none  [the longest x2 79.6 us: shards(): lax.all_to_all(packed.reshape(cluster_count, -1), 'cluster', split_axis=0...]
    pallas_call x0 -> x1, Pallas kernels: none -> 74.5 us  [shards(): pl.pallas_call(kernel, out_shape=jax.ShapeDtypeStruct((TILES * TB, SLICE)...]
    unnamed x2 -> x0, waiting for transfers between devices: 66 us -> none
    all_gather x3 -> x0, blocking collectives: 43 us -> none  [the longest x2 26.9 us: combined_all(): everything = jax.tree.map(lambda part: lax.all_gather(part, axis), shard)]
    unnamed x11 -> x1, local copies, waits for them, and re-layouts: 38.4 us -> 1.63 us
    convert_element_type x11 -> x0, other arithmetic: 24 us -> none  [the longest x8 21.8 us: partial_block(): weight.astype(jnp.bfloat16)]
  transfers between devices with their start and end apart: 5 -> 0, of which waited for: 4 -> 0; matrix products, arithmetic and copies ran while one was open for 1% -> 0% of each run, Pallas kernels for 0% -> 0%
where the time goes in v1:
time: 78.7 us; the launch traced here: 78.5 us
  Pallas kernels  74.5 us (95%)
  local copies, waits for them, and re-layouts  3.28 us (4%)
    pallas_call x1, Pallas kernels, shards(): pl.pallas_call(kernel, out_shape=jax.ShapeDtypeStruct((TILES * TB, SLICE)...  74.5 us
    pallas_call x1, local copies, waits for them, and re-layouts, shards(): pl.pallas_call(kernel, out_shape=jax.ShapeDtypeStruct((TILES * TB, SLICE)...  1.64 us
    unnamed x1, local copies, waits for them, and re-layouts  1.63 us

profile of v1, /device:TPU:1, one launch (start us, length us, event | category | flops | bytes accessed | tf_op | source)
XLA Modules:
  0.0 78.5 jit_solution(14161157066151347688)
XLA Ops:
  0.7 1.6 %copy.7.q_ref = bf16[512,96]{1,0:T(8,128)(2,1)} copy(bf16[512,96]{0,1:T(8,128)(2,1)} %param.6) | data formatting | bytes 196608 | tf_op args[0]
  2.3 74.5 %shard_map.64 = bf16[512,96]{1,0:T(8,128)(2,1)} custom-call(bf16[512,96]{1,0:T(8,128)(2,1)} %copy.7.q_ref, s32[4,4]{1,0:T(4,128)} %probes_ref.1, f32[1,16]{1,0:T(1,128)} %scale_ref.1, s32[1]{0:T(128)S(6)} %copy.9.tiles_ref, bf16[1,2048,768]{2,1,0:T(8,128)(2,1)} %k_hbm.1, bf16[1,2048,768]{2,1,0:T(8,128)(2,1)} %v_hbm.1), custom_call_target="tpu_custom_call" | custom-call | tf_op jit(solution)/shard_map/pallas_call | solution.py:340
  76.8 1.6 %copy.8 = bf16[512,96]{0,1:T(8,128)(2,1)} copy(bf16[512,96]{1,0:T(8,128)(2,1)} %shard_map.64) | data formatting | bytes 196608 | tf_op jit(solution)/shard_map/pallas_call | solution.py:340

commit v2 on v1

v2 whole, which is shorter than its diff:
```python
import math

import jax
import jax.numpy as jnp
from jax import lax
from jax.experimental import pallas as pl
from jax.experimental.pallas import tpu as pltpu
from jax.sharding import PartitionSpec as P

D = 768
TB = 128
KB = 128
PROBE = 4
TILES = 4
CLUSTERS = 16
CAP = 2
SIDE = 4
SLICE = 96
KEYS = 2048
CHUNK = 256
HALF = SIDE * SLICE
STAT = 16
PAIRS = CLUSTERS // 2
FAR = 2
NEAR = PAIRS - FAR
WIDE = 2 * SLICE
MASKED = -1e30
MESH = pl.DeviceIdType.MESH
BF16, F32 = jnp.bfloat16, jnp.float32

ORDER = (
    ((1, 1), (3, 3)),
    ((1, 3), (3, 1)),
    ((1, 2), (3, 0)),
    ((3, 2), (1, 0)),
    ((2, 1), (0, 3)),
    ((2, 3), (0, 1)),
    ((2, 2), (0, 2)),
    ((2, 0), (0, 0)),
)


def shifted(cluster, dy, dx):
    return lax.rem(cluster // SIDE + dy, SIDE) * SIDE + lax.rem(lax.rem(cluster, SIDE) + dx, SIDE)


def picked(values, index):
    code = sum(v * 4**i for i, v in enumerate(values))
    return lax.rem(lax.shift_right_logical(jnp.int32(code), 2 * index), 4)


def terms(x):
    high = x.astype(BF16).astype(F32)
    rest = x - high
    middle = rest.astype(BF16).astype(F32)
    low = (rest - middle).astype(BF16).astype(F32)
    row = lax.broadcasted_iota(jnp.int32, (STAT, x.shape[1]), 0)
    return jnp.where(
        row == 0, high, jnp.where(row == 1, middle, jnp.where(row == 2, low, 0.0))
    ).astype(BF16)


def whole(stat):
    s = stat.astype(F32)
    return s[0:1] + s[1:2] + s[2:3]


def joined(parts, logs):
    top = logs[0]
    for x in logs[1:]:
        top = jnp.maximum(top, x)
    total, mass = None, None
    for part, x in zip(parts, logs):
        w = jnp.exp2(x - top)
        term = part.astype(F32) * w
        total = term if total is None else total + term
        mass = w if mass is None else mass + w
    return total / mass, top + jnp.log2(mass)


def kernel(
    q_ref, probes_ref, scale_ref, tiles_ref, k_hbm, v_hbm, out_ref,
    q_t, pack, qbuf, keys, vals, vt, raw, gain, bias, qp, s_a, s_b, acc, answer, logs,
    osend, rbuf, xsend, xbuf, zsend, zbuf, fsend, fbuf,
    load_sem, pack_sem, send_sem, p1_sem, left_sem, right_sem, far_sem, kv_sem, ret_sem, x_sem, z_sem, f_sem,
):
    c, k = lax.axis_index("cluster"), lax.axis_index("kshard")
    z, core = k // 2, lax.rem(k, 2)
    other = 1 - core
    sibling = (c, 2 * z + other)

    def column(dz):
        return (c, 2 * lax.rem(z + dz, SIDE) + core)

    k_load = pltpu.make_async_copy(k_hbm.at[0], keys.at[core], load_sem.at[0])
    v_load = pltpu.make_async_copy(v_hbm.at[0], vals, load_sem.at[1])
    k_load.start()
    v_load.start()

    barrier = pltpu.get_barrier_semaphore()

    def greet(i, carry):
        d = lax.rem(2 * c + core + i, 2 * CLUSTERS)
        pl.semaphore_signal(
            barrier, inc=1, device_id=(d // 2, 2 * z + lax.rem(d, 2)), device_id_type=MESH
        )
        return carry

    lax.fori_loop(1, 2 * CLUSTERS, greet, 0)
    for dz in range(1, SIDE):
        pl.semaphore_signal(barrier, inc=1, device_id=column(dz), device_id_type=MESH)

    for t in range(TILES):
        q_t[t] = q_ref[:, t * TB : (t + 1) * TB]

    def fill(cc, carry):
        seen, first, second = jnp.int32(0), jnp.int32(0), jnp.int32(0)
        for t in range(TILES):
            hit = jnp.int32(0)
            for p in range(PROBE):
                hit = hit + jnp.where(probes_ref[t, p] == cc, 1, 0)
            first = first + t * hit * jnp.where(seen == 0, 1, 0)
            second = second + t * hit * jnp.where(seen == 1, 1, 0)
            seen = seen + hit
        pack[cc, 0] = q_t[first]
        pack[cc, 1] = q_t[second]
        return carry

    lax.fori_loop(0, CLUSTERS, fill, 0)

    for b in range(KEYS // KB):
        raw[core, b : b + 1, :] = jnp.full((1, 2 * TB), scale_ref[0, b], F32)

    far_clusters = [shifted(c, *ORDER[NEAR + n // 2][n % 2]) for n in range(2 * FAR)]
    stand_in = CAP * shifted(c, *ORDER[0][0])
    places = []
    for t in range(TILES):
        row = []
        for p in range(PROBE):
            cc = probes_ref[t, p]
            slot = jnp.int32(0)
            for before in range(t):
                for other_p in range(PROBE):
                    slot = slot + jnp.where(probes_ref[before, other_p] == cc, 1, 0)
            slot = jnp.minimum(slot, CAP - 1)
            far, number = jnp.int32(0), jnp.int32(0)
            for n, f in enumerate(far_clusters):
                hit = jnp.where(f == cc, 1, 0)
                far, number = far + hit, number + n * hit
            row.append((
                jnp.where(far == 1, stand_in, CAP * cc + slot),
                CAP * number + slot,
                jnp.where(far == 1, MASKED, 0.0),
                jnp.where(far == 1, 0.0, MASKED),
            ))
        places.append(row)

    pl.semaphore_wait(barrier, 2 * CLUSTERS - 1 + SIDE - 1)

    for i in range(CLUSTERS):
        dy, dx = ORDER[i // 2][i % 2]
        cc = shifted(c, dy, dx)
        for s in range(CAP):
            remote = pltpu.make_async_remote_copy(
                src_ref=pack.at[cc, s], dst_ref=qbuf.at[i, k],
                send_sem=pack_sem, recv_sem=p1_sem.at[i],
                device_id=(cc, 2 * z + s), device_id_type=MESH,
            )
            if dy == 0 and dx == 0:
                @pl.when(core == s)
                def _():
                    pltpu.make_async_copy(pack.at[cc, s], qbuf.at[i, k], p1_sem.at[i]).start()

                @pl.when(core != s)
                def _():
                    remote.start()
            else:
                remote.start()

    k_send = pltpu.make_async_remote_copy(
        src_ref=k_hbm.at[0], dst_ref=keys.at[core], send_sem=kv_sem.at[0],
        recv_sem=kv_sem.at[1], device_id=sibling, device_id_type=MESH,
    )
    k_send.start()
    raw_send = pltpu.make_async_remote_copy(
        src_ref=raw.at[core], dst_ref=raw.at[core], send_sem=kv_sem.at[2],
        recv_sem=kv_sem.at[3], device_id=sibling, device_id_type=MESH,
    )
    raw_send.start()

    def turn(b, carry):
        rows = pl.ds(pl.multiple_of(b * 256, 256), 256)
        vt[core, :, rows] = vals[rows, :].T
        return carry

    left, right = lax.rem(z + SIDE - 1, SIDE), lax.rem(z + 1, SIDE)

    def spread(i):
        mine = qbuf.at[i, pl.ds(2 * z, 2)]
        pltpu.make_async_copy(mine, mine, p1_sem.at[i]).wait()
        for arrival, target in ((left_sem, right), (right_sem, left)):
            pltpu.make_async_remote_copy(
                src_ref=mine, dst_ref=mine, send_sem=send_sem.at[1], recv_sem=arrival.at[i],
                device_id=(c, 2 * target + core), device_id_type=MESH,
            ).start()

    def forward(i):
        for arrival, source, target, n in ((left_sem, left, right, 0), (right_sem, right, left, 1)):
            both = qbuf.at[i, pl.ds(2 * source, 2)]
            pltpu.make_async_copy(both, both, arrival.at[i]).wait()
            one = qbuf.at[i, 2 * source + n]
            pltpu.make_async_remote_copy(
                src_ref=one, dst_ref=one, send_sem=send_sem.at[1], recv_sem=far_sem.at[i],
                device_id=(c, 2 * target + core), device_id_type=MESH,
            ).start()

    for i in range(4):
        spread(i)
    v_load.wait()
    lax.fori_loop(0, KEYS // 256, turn, 0)
    v_send = pltpu.make_async_remote_copy(
        src_ref=vt.at[core], dst_ref=vt.at[core], send_sem=kv_sem.at[4],
        recv_sem=kv_sem.at[5], device_id=sibling, device_id_type=MESH,
    )
    v_send.start()
    for i in range(4, 6):
        spread(i)
    for i in range(2):
        forward(i)

    k_load.wait()
    raw_send.wait()
    for h in range(2):
        block = lax.broadcasted_iota(jnp.int32, (KEYS // KB, 2 * TB), 0)
        live = block + (2 * z + h) * (KEYS // KB) < tiles_ref[0]
        gain[h] = jnp.where(live, raw[h] * (math.log2(math.e) / math.sqrt(D)), 0.0)
        bias[h] = jnp.where(live, 0.0, MASKED)

    parts = [(h, j) for h in (core, other) for j in range(KEYS // CHUNK)]

    def scored(part, s_ref):
        h, j = part
        s = jnp.dot(
            keys[h, j * CHUNK : (j + 1) * CHUNK, :], qp[...], preferred_element_type=F32
        )
        top = None
        for b in range(CHUNK // KB):
            row = slice(j * CHUNK // KB + b, j * CHUNK // KB + b + 1)
            x = s[b * KB : (b + 1) * KB] * gain[h, row, :] + bias[h, row, :]
            s_ref[b * KB : (b + 1) * KB, :] = x
            high = jnp.max(x, axis=0, keepdims=True)
            top = high if top is None else jnp.maximum(top, high)
        return top

    def visit(pair, carry):
        @pl.when(pair < PAIRS - 1)
        def _():
            for u in range(2):
                forward(2 * pair + 2 + u)

        @pl.when(pair < PAIRS - 3)
        def _():
            for u in range(2):
                spread(2 * pair + 6 + u)

        for u in range(2):
            i = 2 * pair + u
            rest = qbuf.at[i, pl.ds(0, 2)]
            pltpu.make_async_copy(rest, rest, far_sem.at[i]).wait()
            qp[:, u * TB : (u + 1) * TB] = qbuf[i].reshape(D, TB)

        buffers = (s_a, s_b)
        top = scored(parts[0], buffers[0])
        best, mass = None, None
        for n, (h, j) in enumerate(parts):
            if n + 1 == len(parts) // 2:

                @pl.when(pair == 0)
                def _():
                    k_send.wait()
                    v_send.wait()

            if n + 1 < len(parts):
                next_top = scored(parts[n + 1], buffers[(n + 1) % 2])
            now = top if best is None else jnp.maximum(best, top)
            weight = jnp.exp2(buffers[n % 2][...] - now)
            row_sum = jnp.sum(weight, axis=0, keepdims=True)
            mixture = jnp.dot(
                vt[h, :, j * CHUNK : (j + 1) * CHUNK], weight.astype(BF16),
                preferred_element_type=F32,
            )
            if best is None:
                acc[...] = mixture
                mass = row_sum
            else:
                fade = jnp.exp2(best - now)
                acc[...] = acc[...] * fade + mixture
                mass = mass * fade + row_sum
            best = now
            if n + 1 < len(parts):
                top = next_top

        answer[...] = (acc[...] * (1.0 / mass)).astype(BF16)
        logs[...] = terms(best + jnp.log2(mass))

        @pl.when(pair < NEAR)
        def _():
            for u in range(2):
                i = 2 * pair + u
                lanes = slice(u * TB, (u + 1) * TB)
                for half in range(2):
                    for part in range(SIDE):
                        first = (2 * part + half) * SLICE
                        osend[i, half, part * SLICE : (part + 1) * SLICE, :] = answer[
                            first : first + SLICE, lanes
                        ]
                    osend[i, half, HALF : HALF + STAT, :] = logs[:, lanes]
            for u in range(2):
                i = 2 * pair + u
                dy = picked([(SIDE - ORDER[n][u][0]) % SIDE for n in range(PAIRS)], pair)
                dx = picked([(SIDE - ORDER[n][u][1]) % SIDE for n in range(PAIRS)], pair)
                for half in range(2):
                    pltpu.make_async_remote_copy(
                        src_ref=osend.at[i, half], dst_ref=rbuf.at[CAP * c + core],
                        send_sem=send_sem.at[2], recv_sem=ret_sem,
                        device_id=(shifted(c, dy, dx), 2 * z + half), device_id_type=MESH,
                    ).start()

        @pl.when(pair >= NEAR)
        def _():
            for u in range(2):
                n = 2 * (pair - NEAR) + u
                lanes = slice(u * TB, (u + 1) * TB)
                for part in range(SIDE):
                    zsend[n, part, 0:WIDE, :] = answer[part * WIDE : (part + 1) * WIDE, lanes]
                    zsend[n, part, WIDE : WIDE + STAT, :] = logs[:, lanes]
            for u in range(2):
                n = 2 * (pair - NEAR) + u
                for dz in (2, 1, 3):
                    pltpu.make_async_remote_copy(
                        src_ref=zsend.at[n, lax.rem(z + dz, SIDE)], dst_ref=zbuf.at[n, z],
                        send_sem=send_sem.at[0], recv_sem=z_sem.at[n], device_id=column(dz),
                        device_id_type=MESH,
                    ).start()

        return carry

    lax.fori_loop(0, PAIRS, visit, 0)

    def settle(n):
        three = zsend.at[n, pl.ds(0, 3)]
        pltpu.make_async_copy(three, three, z_sem.at[n]).wait()
        found = [zsend[n, z]] + [zbuf[n, lax.rem(z + dz, SIDE)] for dz in range(1, SIDE)]
        total, log = joined([x[0:WIDE] for x in found], [whole(x[WIDE : WIDE + STAT]) for x in found])
        stat = terms(log)
        dy, dx = ORDER[NEAR + n // 2][n % 2]
        g = shifted(c, (SIDE - dy) % SIDE, (SIDE - dx) % SIDE)
        for half in range(2):
            fsend[2 * n + half, 0:SLICE, :] = total[half * SLICE : (half + 1) * SLICE].astype(BF16)
            fsend[2 * n + half, SLICE : SLICE + STAT, :] = stat
        for half in range(2):
            source, target = fsend.at[2 * n + half], fbuf.at[CAP * n + core]
            remote = pltpu.make_async_remote_copy(
                src_ref=source, dst_ref=target, send_sem=send_sem.at[4], recv_sem=f_sem,
                device_id=(g, 2 * z + half), device_id_type=MESH,
            )
            if dy == 0 and dx == 0:

                @pl.when(core == half)
                def _():
                    pltpu.make_async_copy(source, target, f_sem).start()

                @pl.when(core != half)
                def _():
                    remote.start()
            else:
                remote.start()

    settle(0)
    settle(1)

    arrived = rbuf.at[pl.ds(0, 4 * NEAR)]
    pltpu.make_async_copy(arrived, arrived, ret_sem).wait()
    for t in range(TILES):
        logs_t = [whole(rbuf[f, HALF : HALF + STAT, :]) + m for f, _, m, _ in places[t]]
        total, log = joined([rbuf[f, 0:HALF, :] for f, _, _, _ in places[t]], logs_t)
        stat = terms(log)
        for part in range(SIDE):
            xsend[part, t, 0:SLICE, :] = total[part * SLICE : (part + 1) * SLICE].astype(BF16)
            xsend[part, t, SLICE : SLICE + STAT, :] = stat
        for dz in (2, 1, 3):
            pltpu.make_async_remote_copy(
                src_ref=xsend.at[lax.rem(z + dz, SIDE), t], dst_ref=xbuf.at[z, t],
                send_sem=send_sem.at[3], recv_sem=x_sem.at[t], device_id=column(dz),
                device_id_type=MESH,
            ).start()
        xbuf[z, t] = xsend[z, t]

    settle(2)
    settle(3)

    pltpu.make_async_copy(fbuf, fbuf, f_sem).wait()
    for t in range(TILES):
        three = xsend.at[pl.ds(0, 3), t]
        pltpu.make_async_copy(three, three, x_sem.at[t]).wait()
        found = [xbuf[n, t] for n in range(SIDE)]
        logs_t = [whole(x[SLICE : SLICE + STAT]) for x in found]
        for _, f, _, m in places[t]:
            found.append(fbuf[f])
            logs_t.append(whole(found[-1][SLICE : SLICE + STAT]) + m)
        total, _ = joined([x[0:SLICE] for x in found], logs_t)
        out_ref[:, t * TB : (t + 1) * TB] = total.astype(BF16)

    flat_pack = pack.at[pl.ds(0, 15)]
    pltpu.make_async_copy(flat_pack, flat_pack, pack_sem).wait()
    pltpu.make_async_copy(pack.at[0, 0], pack.at[0, 0], pack_sem).wait()
    relayed = qbuf.at[pl.ds(0, 12)]
    pltpu.make_async_copy(relayed, relayed, send_sem.at[1]).wait()
    pltpu.make_async_copy(osend, osend, send_sem.at[2]).wait()
    three = zsend.at[pl.ds(0, 3)]
    pltpu.make_async_copy(three, three, send_sem.at[0]).wait()
    pltpu.make_async_copy(xsend.at[pl.ds(0, 3)], xsend.at[pl.ds(0, 3)], send_sem.at[3]).wait()
    seven = fsend.at[pl.ds(0, 7)]
    pltpu.make_async_copy(seven, seven, send_sem.at[4]).wait()


def shards(queries, probes, key_rows, value_rows, key_scale, key_tiles):
    vmem = pl.BlockSpec(memory_space=pltpu.VMEM)
    smem = pl.BlockSpec(memory_space=pltpu.SMEM)
    hbm = pl.BlockSpec(memory_space=pl.ANY)
    dma = pltpu.SemaphoreType.DMA
    return pl.pallas_call(
        kernel,
        out_shape=jax.ShapeDtypeStruct((SLICE, TILES * TB), BF16),
        in_specs=[vmem, smem, smem, smem, hbm, hbm],
        out_specs=vmem,
        scratch_shapes=[
            pltpu.VMEM((TILES, SLICE, TB), BF16),
            pltpu.VMEM((CLUSTERS, CAP, SLICE, TB), BF16),
            pltpu.VMEM((CLUSTERS, 2 * SIDE, SLICE, TB), BF16),
            pltpu.VMEM((2, KEYS, D), BF16),
            pltpu.VMEM((KEYS, D), BF16),
            pltpu.VMEM((2, D, KEYS), BF16),
            pltpu.VMEM((2, KEYS // KB, 2 * TB), F32),
            pltpu.VMEM((2, KEYS // KB, 2 * TB), F32),
            pltpu.VMEM((2, KEYS // KB, 2 * TB), F32),
            pltpu.VMEM((D, 2 * TB), BF16),
            pltpu.VMEM((CHUNK, 2 * TB), F32),
            pltpu.VMEM((CHUNK, 2 * TB), F32),
            pltpu.VMEM((D, 2 * TB), F32),
            pltpu.VMEM((D, 2 * TB), BF16),
            pltpu.VMEM((STAT, 2 * TB), BF16),
            pltpu.VMEM((2 * NEAR, 2, HALF + STAT, TB), BF16),
            pltpu.VMEM((CAP * CLUSTERS, HALF + STAT, TB), BF16),
            pltpu.VMEM((SIDE, TILES, SLICE + STAT, TB), BF16),
            pltpu.VMEM((SIDE, TILES, SLICE + STAT, TB), BF16),
            pltpu.VMEM((2 * FAR, SIDE, WIDE + STAT, TB), BF16),
            pltpu.VMEM((2 * FAR, SIDE, WIDE + STAT, TB), BF16),
            pltpu.VMEM((4 * FAR, SLICE + STAT, TB), BF16),
            pltpu.VMEM((4 * FAR, SLICE + STAT, TB), BF16),
            dma((2,)),
            dma,
            dma((5,)),
            dma((CLUSTERS,)),
            dma((CLUSTERS,)),
            dma((CLUSTERS,)),
            dma((CLUSTERS,)),
            dma((6,)),
            dma,
            dma((TILES,)),
            dma((2 * FAR,)),
            dma,
        ],
        compiler_params=pltpu.CompilerParams(
            collective_id=0, has_side_effects=True, vmem_limit_bytes=60 * 2**20
        ),
    )(queries.T, probes, key_scale, key_tiles, key_rows, value_rows).T


def solution(mesh):
    return jax.shard_map(
        shards,
        mesh=mesh,
        in_specs=(
            P("cluster", "kshard"),
            P("cluster", None),
            P("cluster", "kshard", None),
            P("cluster", "kshard", None),
            P("cluster", "kshard"),
            P("cluster"),
        ),
        out_specs=P("cluster", "kshard"),
        check_vma=False,
    )
```

time: 78.7 us -> 74.8 us (0.950)
  Pallas kernels: 74.5 us -> 72.5 us
  local copies, waits for them, and re-layouts: 3.28 us -> 1.54 us
    pallas_call x1, Pallas kernels: 74.5 us -> 72.5 us  [shards(): pl.pallas_call(kernel, out_shape=jax.ShapeDtypeStruct((SLICE, TILES * TB)...]
    pallas_call x1 -> x0, local copies, waits for them, and re-layouts: 1.64 us -> none  [shards(): pl.pallas_call(kernel, out_shape=jax.ShapeDtypeStruct((TILES * TB, SLICE)...]
where the time goes in v2:
time: 74.8 us; the launch traced here: 74.7 us
  Pallas kernels  72.5 us (97%)
  local copies, waits for them, and re-layouts  1.54 us (2%)
    pallas_call x1, Pallas kernels, shards(): pl.pallas_call(kernel, out_shape=jax.ShapeDtypeStruct((SLICE, TILES * TB)...  72.5 us
    unnamed x1, local copies, waits for them, and re-layouts  1.54 us

profile of v2, /device:TPU:1, one launch (start us, length us, event | category | flops | bytes accessed | tf_op | source)
XLA Modules:
  0.0 74.7 jit_solution(8145536666379347376)
XLA Ops:
  0.7 72.5 %shard_map.64 = bf16[96,512]{1,0:T(8,128)(2,1)} custom-call(bf16[96,512]{1,0:T(8,128)(2,1)} %bitcast.3, s32[4,4]{1,0:T(4,128)} %probes_ref.1, f32[1,16]{1,0:T(1,128)} %scale_ref.1, s32[1]{0:T(128)S(6)} %copy.8.tiles_ref, bf16[1,2048,768]{2,1,0:T(8,128)(2,1)} %k_hbm.1, bf16[1,2048,768]{2,1,0:T(8,128)(2,1)} %v_hbm.1), custom_call_target="tpu_custom_call" | custom-call | tf_op jit(solution)/shard_map/pallas_call | solution.py:432
  73.1 1.5 %copy.9 = bf16[512,96]{0,1:T(8,128)(2,1)} copy(bf16[512,96]{0,1:T(8,128)(2,1)} %bitcast.2) | data formatting | bytes 196608

commit v3 on v2

--- a/solution.py
+++ b/solution.py
@@ -214,7 +214,7 @@
                 device_id=(c, 2 * target + core), device_id_type=MESH,
             ).start()
 
-    for i in range(4):
+    for i in range(2):
         spread(i)
     v_load.wait()
     lax.fori_loop(0, KEYS // 256, turn, 0)
@@ -223,10 +223,10 @@
         recv_sem=kv_sem.at[5], device_id=sibling, device_id_type=MESH,
     )
     v_send.start()
-    for i in range(4, 6):
-        spread(i)
     for i in range(2):
         forward(i)
+    for i in range(2, 6):
+        spread(i)
 
     k_load.wait()
     raw_send.wait()
@@ -376,9 +376,6 @@
             else:
                 remote.start()
 
-    settle(0)
-    settle(1)
-
     arrived = rbuf.at[pl.ds(0, 4 * NEAR)]
     pltpu.make_async_copy(arrived, arrived, ret_sem).wait()
     for t in range(TILES):
@@ -396,8 +393,8 @@
             ).start()
         xbuf[z, t] = xsend[z, t]
 
-    settle(2)
-    settle(3)
+    for n in range(2 * FAR):
+        settle(n)
 
     pltpu.make_async_copy(fbuf, fbuf, f_sem).wait()
     for t in range(TILES):
@@ -420,7 +417,7 @@
     three = zsend.at[pl.ds(0, 3)]
     pltpu.make_async_copy(three, three, send_sem.at[0]).wait()
     pltpu.make_async_copy(xsend.at[pl.ds(0, 3)], xsend.at[pl.ds(0, 3)], send_sem.at[3]).wait()
-    seven = fsend.at[pl.ds(0, 7)]
+    seven = fsend.at[pl.ds(0, 4 * FAR - 1)]
     pltpu.make_async_copy(seven, seven, send_sem.at[4]).wait()
 
 

time: 74.8 us -> 74.4 us (level); the launches traced: 74.7 us -> 73.4 us
  Pallas kernels: 72.5 us -> 71.2 us
    pallas_call x1, Pallas kernels: 72.5 us -> 71.2 us  [shards(): pl.pallas_call(kernel, out_shape=jax.ShapeDtypeStruct((SLICE, TILES * TB)...]
where the time goes in v3:
time: 74.4 us; the launch traced here: 73.4 us
  Pallas kernels  71.2 us (96%)
  local copies, waits for them, and re-layouts  1.54 us (2%)
    pallas_call x1, Pallas kernels, shards(): pl.pallas_call(kernel, out_shape=jax.ShapeDtypeStruct((SLICE, TILES * TB)...  71.2 us
    unnamed x1, local copies, waits for them, and re-layouts  1.54 us

profile of v3, /device:TPU:1, one launch (start us, length us, event | category | flops | bytes accessed | tf_op | source)
XLA Modules:
  0.0 73.4 jit_solution(4321881100589200988)
XLA Ops:
  0.7 71.2 %shard_map.64 = bf16[96,512]{1,0:T(8,128)(2,1)} custom-call(bf16[96,512]{1,0:T(8,128)(2,1)} %bitcast.3, s32[4,4]{1,0:T(4,128)} %probes_ref.1, f32[1,16]{1,0:T(1,128)} %scale_ref.1, s32[1]{0:T(128)S(6)} %copy.8.tiles_ref, bf16[1,2048,768]{2,1,0:T(8,128)(2,1)} %k_hbm.1, bf16[1,2048,768]{2,1,0:T(8,128)(2,1)} %v_hbm.1), custom_call_target="tpu_custom_call" | custom-call | tf_op jit(solution)/shard_map/pallas_call | solution.py:429
  71.9 1.5 %copy.9 = bf16[512,96]{0,1:T(8,128)(2,1)} copy(bf16[512,96]{0,1:T(8,128)(2,1)} %bitcast.2) | data formatting | bytes 196608
